TPU v7x, 256 devices: a whole 4x4x8 slice. The times are simulated.
256 devices in a mesh: grp: 16 (over y_hi, x, core), tp: 16 (over y_lo, z).
Axes of the slice: x: 4, y: 4 (y_hi: 2, y_lo: 2; y = y_hi * 2 + y_lo), z: 8, core: 2. Of those that a mesh axis runs over, the one named last changes fastest.
Arguments:
- x_rows: bfloat16 [16384, 4096], P(('grp', 'tp')), may hold values from -6 to 6
- norm_gain: float32 [4096], replicated, may hold values from 0.1 to 1.9
- w_query: bfloat16 [4096, 4096], P(None, 'tp'), may hold values from -0.25 to 0.25
- w_keyval: bfloat16 [4096, 2, 1024], P(None, None, 'tp'), may hold values from -0.09375 to 0.09375
- w_out: bfloat16 [4096, 4096], P('tp'), may hold values from -0.75 to 0.75
- prefix_cache: bfloat16 [32, 128, 2, 1024], P('grp', None, None, 'tp'), may hold values from -70 to 70, as said below
- page_table: int32 [32], replicated, may hold values from 0 to 31, each once
- request_ids: int32 [16384], replicated, may hold values from 0 to 31, never falling along the last dimension, each value on 1 to 1024 neighbouring positions
Outputs:
- attn_out: bfloat16 [16384, 4096], P(('grp', 'tp'))
Inputs may be any that keep to these rules, and one draw needn't show every extreme that they name: `request_ids`: request ids never fall along the stream; each of the 32 requests has 1 to 1024 tokens, one exactly 1024. `page_table`: a permutation; physical page f belongs to group f // 2. `prefix_cache`: keys are stored already rotated for their positions.
All inputs are finite; a program needn't handle non-finite values.
Results may differ from a plain program's by a relative error of at most 0.025.
The roundings to bfloat16 on the way count: a program that leaves them out, or rounds other values in their place, can miss the bound.
Values may be sent and summed in bfloat16 or wider, within the bound.
A program may use at most 64 MiB of HBM per device.

v0:
```python
import jax
import jax.numpy as jnp
from jax import lax
from jax.sharding import PartitionSpec as P

KVH = 8
HD = 128
SINKS = 4


def swapped(block, axis, apart):
    count = lax.axis_size(axis)
    route = []
    for low in range(count):
        high = low | 1 << apart
        if high != low and high < count:
            route += [(low, high), (high, low)]
    return lax.ppermute(block, axis, route)


def shifted(block, axis, distance):
    devices = range(lax.axis_size(axis))
    route = [(i - distance, i) for i in devices if i - distance in devices]
    return lax.ppermute(block, axis, route)


def rotate(values, positions):
    half = HD // 2
    freqs = 500000.0 ** (-jnp.arange(half, dtype=jnp.float32) * 2.0 / HD)
    angles = positions.astype(jnp.float32)[:, None] * freqs[None, :]
    cosine = jnp.cos(angles)[:, None, :]
    sine = jnp.sin(angles)[:, None, :]
    first = values[..., :half]
    second = values[..., half:]
    return jnp.concatenate(
        [first * cosine - second * sine, second * cosine + first * sine], axis=-1
    )


def segment_first(request_ids, wanted, count):
    labels = jnp.arange(count, dtype=jnp.int32)
    counts = jnp.sum((request_ids[:, None] == labels[None, :]).astype(jnp.int32), axis=0)
    starts = jnp.cumsum(counts) - counts
    match = wanted[:, None] == labels[None, :]
    return jnp.sum(jnp.where(match, starts[None, :], 0), axis=1)


def join_pair(lower, mine, peer):
    return jnp.where(
        lower, jnp.concatenate([mine, peer], axis=2), jnp.concatenate([peer, mine], axis=2)
    )


def fold_block(state, queries, keys, values, visible):
    run_max, run_sum, run_acc = state
    scores = jnp.einsum(
        "qgrd,kgd->qgrk", queries, keys, preferred_element_type=jnp.float32
    ) * HD ** (-0.5)
    allowed = visible[:, None, None, :]
    scores = jnp.where(allowed, scores, -1e30)
    new_max = jnp.maximum(run_max, jnp.max(scores, axis=-1))
    weights = jnp.where(allowed, jnp.exp(scores - new_max[..., None]), 0.0)
    factor = jnp.exp(run_max - new_max)
    new_sum = run_sum * factor + jnp.sum(weights, axis=-1)
    new_acc = run_acc * factor[..., None] + jnp.einsum(
        "qgrk,kgd->qgrd", weights.astype(jnp.bfloat16), values, preferred_element_type=jnp.float32
    )
    return (new_max, new_sum, new_acc)


def fold_all(
    state, queries, query_pos, query_seg, query_index, keys, values, visible_fn, block_rows
):
    blocks = queries.shape[0] // block_rows

    def in_blocks(array):
        return array.reshape((blocks, block_rows) + array.shape[1:])

    def update_block(item):
        part_state, part_queries, part_pos, part_seg, part_index = item
        return fold_block(
            part_state, part_queries, keys, values, visible_fn(part_pos, part_seg, part_index)
        )

    pieces = (
        tuple((in_blocks(member) for member in state)),
        in_blocks(queries),
        in_blocks(query_pos),
        in_blocks(query_seg),
        in_blocks(query_index),
    )
    result = lax.map(update_block, pieces)
    return tuple((member.reshape((-1,) + member.shape[2:]) for member in result))


def local(x_rows, norm_gain, w_query, w_keyval, w_out, prefix_cache, page_table, request_ids):
    tp_size = lax.axis_size("tp")
    grp_size = lax.axis_size("grp")
    tp_index = lax.axis_index("tp")
    grp_index = lax.axis_index("grp")
    tok_dev = x_rows.shape[0]
    tok_group = tok_dev * tp_size
    heads_dev = w_query.shape[1] // HD
    kv_cols = w_keyval.shape[2]
    kv_need = max(HD, HD * KVH // tp_size)
    kv_heads = kv_need // HD
    per_kv = heads_dev // kv_heads
    pages_dev = prefix_cache.shape[0]
    page_len = prefix_cache.shape[1]
    prefix_len = pages_dev * grp_size * page_len
    seg_count = 2 * grp_size
    block_rows = min(512, tok_group)
    wide = x_rows.astype(jnp.float32)
    variance = jnp.mean(wide * wide, axis=-1, keepdims=True) + 1e-05
    inverse = lax.rsqrt(variance)
    normed = (wide * inverse * norm_gain).astype(jnp.bfloat16)
    kv_weight = w_keyval.reshape(w_keyval.shape[0], 2 * kv_cols)
    piece = lax.all_gather(normed, "tp", axis=0, tiled=True)
    query_part = jnp.dot(piece, w_query, preferred_element_type=jnp.float32)
    kv_part = jnp.dot(piece, kv_weight, preferred_element_type=jnp.float32)
    projected = jnp.concatenate([query_part, kv_part], axis=1)
    query_cols = heads_dev * HD
    group_start = grp_index * tok_group
    token_index = group_start + jnp.arange(tok_group, dtype=jnp.int32)
    own_seg = lax.dynamic_slice_in_dim(request_ids, group_start, tok_group, 0)
    own_pos = prefix_len + token_index - segment_first(request_ids, own_seg, seg_count)
    queries = rotate(projected[:, :query_cols].reshape(tok_group, heads_dev, HD), own_pos).astype(
        jnp.bfloat16
    )
    queries = queries.reshape(tok_group, kv_heads, per_kv, HD)
    kv_local = projected[:, query_cols:].astype(jnp.bfloat16).reshape(tok_group, 2, kv_cols)
    cache_local = prefix_cache.reshape(pages_dev * page_len, 2, kv_cols)
    kv_own = kv_local
    cache_own = cache_local
    kv_peer, cache_peer = swapped((kv_own, cache_own), "tp", 0)
    lower = tp_index >> 0 & 1 == 0
    kv_own = join_pair(lower, kv_own, kv_peer)
    cache_own = join_pair(lower, cache_own, cache_peer)
    keys_own = rotate(
        kv_own[:, 0].reshape(tok_group, kv_heads, HD).astype(jnp.float32), own_pos
    ).astype(jnp.bfloat16)
    values_own = kv_own[:, 1].reshape(tok_group, kv_heads, HD)
    keys_prev, values_prev = shifted((keys_own, values_own), "grp", 1)
    prev_start = jnp.maximum(group_start - tok_group, 0)
    prev_index = group_start - tok_group + jnp.arange(tok_group, dtype=jnp.int32)
    prev_seg = jnp.where(
        grp_index > 0, lax.dynamic_slice_in_dim(request_ids, prev_start, tok_group, 0), -1
    )
    prev_pos = prefix_len + prev_index - segment_first(request_ids, prev_seg, seg_count)
    suffix_keys = jnp.concatenate([keys_prev, keys_own], axis=0)
    suffix_values = jnp.concatenate([values_prev, values_own], axis=0)
    suffix_seg = jnp.concatenate([prev_seg, own_seg], axis=0)
    suffix_pos = jnp.concatenate([prev_pos, own_pos], axis=0)
    suffix_index = jnp.concatenate([prev_index, token_index], axis=0)

    def suffix_visible(query_pos, query_seg, query_index):
        same = (suffix_seg[None, :] == query_seg[:, None]) & (
            suffix_index[None, :] <= query_index[:, None]
        )
        return same & (
            (query_pos[:, None] - suffix_pos[None, :] < prefix_len) | (suffix_pos[None, :] < SINKS)
        )

    start_state = (
        jnp.full((tok_group, kv_heads, per_kv), -1e30, jnp.float32),
        jnp.zeros((tok_group, kv_heads, per_kv), jnp.float32),
        jnp.zeros((tok_group, kv_heads, per_kv, HD), jnp.float32),
    )
    state = fold_all(
        start_state,
        queries,
        own_pos,
        own_seg,
        token_index,
        suffix_keys,
        suffix_values,
        suffix_visible,
        block_rows,
    )
    page_labels = jnp.arange(page_table.shape[0], dtype=jnp.int32)
    cache_keys = cache_own[:, 0].reshape(pages_dev * page_len, kv_heads, HD)
    cache_values = cache_own[:, 1].reshape(pages_dev * page_len, kv_heads, HD)
    piece_keys = lax.all_gather(cache_keys, "grp", axis=0, tiled=True)
    piece_values = lax.all_gather(cache_values, "grp", axis=0, tiled=True)
    rows = piece_keys.shape[0]
    physical = jnp.arange(rows // page_len, dtype=jnp.int32)
    logical = jnp.sum(
        jnp.where(page_table[None, :] == physical[:, None], page_labels[None, :], 0), axis=1
    )
    key_pos = (
        logical[:, None] * page_len + jnp.arange(page_len, dtype=jnp.int32)[None, :]
    ).reshape(rows)

    def prefix_visible(query_pos, query_seg, query_index):
        before = key_pos[None, :] <= query_pos[:, None]
        return before & (
            (query_pos[:, None] - key_pos[None, :] < prefix_len) | (key_pos[None, :] < SINKS)
        )

    state = fold_all(
        state,
        queries,
        own_pos,
        own_seg,
        token_index,
        piece_keys,
        piece_values,
        prefix_visible,
        block_rows,
    )
    attn = (state[2] / state[1][..., None]).reshape(tok_group, heads_dev * HD).astype(jnp.bfloat16)
    rows = attn
    return lax.psum_scatter(
        jnp.dot(rows, w_out, preferred_element_type=jnp.float32).astype(jnp.bfloat16),
        "tp",
        scatter_dimension=0,
        tiled=True,
    )


def solution(mesh):
    placed = (
        P(("grp", "tp"), None),
        P(),
        P(None, "tp"),
        P(None, None, "tp"),
        P("tp", None),
        P("grp", None, None, "tp"),
        P(),
        P(),
    )
    return jax.shard_map(
        local, mesh=mesh, in_specs=placed, out_specs=P(("grp", "tp"), None), check_vma=False
    )
```

profile of v0, /device:TPU:1, one launch (start us, length us, event | category | flops | bytes accessed | tf_op | source)
XLA Modules:
  0.0 373.4 jit_solution(2221443877971759652)
XLA Ops:
  6.5 1.4 fusion.67
  7.9 2.0 fusion.69
  10.1 1.0 copy.36
  11.0 2.6 collective-permute-start.3
  13.6 1.1 convert_reduce_fusion
  14.7 0.1 copy.32
  14.9 0.1 reduce.4
  15.0 0.8 dynamic-slice_select_fusion
  15.9 0.1 collective-permute-done.3
  15.9 0.1 maximum_select_fusion.1
  16.1 0.7 fusion.82
  16.8 0.1 select_reduce_fusion
  17.1 0.8 select_reduce_fusion.2
  17.9 1.0 multiply_cosine_fusion.1
  18.9 96.0 %all-gather.4.cloned.1.call-done = bf16[1024,4096]{1,0:T(8,128)(2,1)} async-done(((bf16[64,4096]{1,0:T(8,128)(2,1)}), bf16[1024,4096]{1,0:T(8,128)(2,1)}) %all-gather.4.cloned.1.call-update) | async-done | bytes 8388624 | tf_op jit(solution)/shard_map/all_gather | solution.py:118
  115.0 6.7 %convolution_convert_fusion.1 = bf16[1024,128]{0,1:T(8,128)(2,1)S(1)} fusion(bf16[1024,4096]{1,0:T(8,128)(2,1)} %all-gather.4.cloned.1.call-done, bf16[4096,128]{0,1:T(8,128)(2,1)} %bitcast.261), kind=kOutput, calls=%fused_computation.79 | convolution fusion | flops 1073872896 | bytes 9699328 | tf_op jit(solution)/shard_map/dot_general | solution.py:120
  121.6 0.1 collective-permute-start
  121.8 2.4 fusion.83
  124.2 4.7 %collective-permute-done = bf16[1024,2,64]{0,2,1:T(8,128)(2,1)S(1)} collective-permute-done((bf16[1024,2,64]{0,2,1:T(8,128)(2,1)S(1)}, bf16[1024,2,64]{0,2,1:T(8,128)(2,1)S(1)}, u32[]{:S(2)}, u32[]{:S(2)}) %collective-permute-start) | collective-permute-done | bytes 262176 | tf_op jit(solution)/shard_map/ppermute | solution.py:18
  128.9 0.1 maximum_select_fusion
  129.1 1.2 fusion.77
  130.3 0.7 pad_maximum_fusion.2
  131.0 4.5 %collective-permute-start.1 = (bf16[1024,1,128]{0,2,1:T(8,128)(2,1)}, bf16[1024,1,128]{0,2,1:T(8,128)(2,1)}, u32[]{:S(2)}, u32[]{:S(2)}) collective-permute-start(bf16[1024,1,128]{0,2,1:T(8,128)(2,1)} %pad_maximum_fusion.2), channel_id=1, source_target_pairs={{0,16},{16,32},{32,48},{48,64},{64,80},{80,96},{96,112},{112,128},... | collective-permute-start | bytes 786440 | tf_op jit(solution)/shard_map/ppermute | solution.py:24
  135.5 0.9 subtract_convert_fusion
  136.4 1.2 concatenate.58
  137.6 0.9 concatenate.57
  138.4 2.1 collective-permute-start.2
  140.6 1.6 pad_maximum_fusion
  142.2 1.1 copy.33
  143.3 1.0 maximum_maximum_fusion
  144.3 1.0 copy.34
  145.3 1.0 pad_maximum_fusion.1
  146.3 0.3 copy.35
  146.6 25.5 %while.27 = (s32[]{:T(128)}, f32[2,512,1,2]{1,3,2,0:T(2,128)S(1)}, f32[2,512,1,2]{1,3,2,0:T(2,128)S(1)}, f32[2,512,1,2,128]{4,1,3,2,0:T(8,128)}, s32[2048]{0:T(1...) while((s32[]{:T(128)}, f32[2,512,1,2]{1,3,2,0:T(2,128)S(1)}, ...), condition=%wide.region_8.9_spmd, body=%wide.region_5.8_spmd.sunk | while | flops 1108483072 | bytes 39688408 | solution.py:92
  146.7 2.1 fusion.106
  148.8 3.2 fusion.107
  152.1 2.9 fusion.108
  155.0 3.4 fusion.110
  158.4 1.0 copy-done.5
  159.4 2.1 fusion.106
  161.6 3.2 fusion.107
  164.8 2.9 fusion.108
  167.7 3.4 fusion.110
  171.1 1.0 copy-done.5
  172.1 45.6 %all-gather.8.cloned.1.call-done = bf16[4096,1,128]{2,0,1:T(8,128)(2,1)} async-done(((bf16[256,1,128]{2,0,1:T(8,128)(2,1)}), bf16[4096,1,128]{2,0,1:T(8,128)(2,1)}) %all-gather.8.cloned.1.call-update) | async-done | bytes 1048592 | tf_op jit(solution)/shard_map/all_gather | solution.py:184
  217.7 41.1 %while.28 = (s32[]{:T(128)}, f32[2,512,1,2]{1,3,2,0:T(2,128)S(1)}, f32[2,512,1,2,128]{4,3,1,0,2:T(2,128)}, f32[2,512,1,2]{1,3,2,0:T(2,128)S(1)}, f32[2,512,1,2]{...) while((s32[]{:T(128)}, f32[2,512,1,2]{1,3,2,0:T(2,128)S(1)}, ...), condition=%wide.region_13.14_spmd.clone, body=%wide.region_10.13_spmd.clone.sunk | while | flops 2212773888 | bytes 71670216 | solution.py:92
  217.7 0.1 add_bitcast_fusion.2
  217.8 0.1 broadcast_compare_fusion.5
  217.9 2.6 fusion.113
  220.5 5.1 %fusion.114 = (f32[512,2]{0,1:T(2,128)S(1)}, f32[512,2,4096]{2,0,1:T(8,128)S(1)}) fusion(pred[512,4096]{1,0:T(8,128)(4,1)S(1)} %fusion.113, bf16[4096,1,128]{2,0,1:T(8,128)(2,1)} %get-tuple-element.555, bf16[2,512,1,2,128]{4,1,3,2,0:T(8,128)(2,1)} %get-tuple-element.554, s32[]{:T(128)S(6)} %copy.72), kind=kOutput, calls=%fused_computation.39.clone.1 | convolution fusion | flops 1086323712 | bytes 20189188 | tf_op jit(solution)/shard_map/while/body/eval_jaxpr/qgrd,kgd->qgrk/dot_general | solution.py:56
  225.7 5.3 %fusion.116 = f32[512,2]{0,1:T(2,128)S(1)} fusion(f32[512,2,4096]{2,0,1:T(8,128)S(1)} %get-tuple-element.478, f32[512,2]{0,1:T(2,128)S(1)} %get-tuple-element.480, pred[512,4096]{1,0:T(8,128)(4,1)S(1)} %fusion.113), kind=kLoop, calls=%fused_computation.41.clone.1 | loop fusion | flops 20970496 | bytes 18882560 | tf_op jit(solution)/shard_map/while/body/eval_jaxpr/reduce_sum | solution.py:64
  231.0 6.0 %fusion.118 = f32[1,512,1,2,128]{4,1,3,2,0:T(8,128)S(1)} fusion(f32[512,2,4096]{2,0,1:T(8,128)S(1)} %get-tuple-element.478, f32[512,2]{0,1:T(2,128)S(1)} %get-tuple-element.480, pred[512,4096]{1,0:T(8,128)(4,1)S(1)} %fusion.113, bf16[4096,1,128]{2,0,1:T(8,128)(2,1)S(1)} %copy-done.3, f32[2,512,1,2,128]{4,1,3,2,0:T(8,128)S(1)} %copy-done.6, ...), kind=kOutput, calls=%fused_computation.50.clone.1 | convolution fusion | flops 1094975488 | bytes 20979716 | tf_op jit(solution)/shard_map/while/body/eval_jaxpr/qgrk,kgd->qgrd/dot_general | solution.py:65
  237.0 1.2 copy_dynamic-update-slice_fusion.2
  238.2 0.1 add_bitcast_fusion.2
  238.3 0.1 broadcast_compare_fusion.5
  238.4 2.6 fusion.113
  241.0 5.1 %fusion.114 = (f32[512,2]{0,1:T(2,128)S(1)}, f32[512,2,4096]{2,0,1:T(8,128)S(1)}) fusion(pred[512,4096]{1,0:T(8,128)(4,1)S(1)} %fusion.113, bf16[4096,1,128]{2,0,1:T(8,128)(2,1)} %get-tuple-element.555, bf16[2,512,1,2,128]{4,1,3,2,0:T(8,128)(2,1)} %get-tuple-element.554, s32[]{:T(128)S(6)} %copy.72), kind=kOutput, calls=%fused_computation.39.clone.1 | convolution fusion | flops 1086323712 | bytes 20189188 | tf_op jit(solution)/shard_map/while/body/eval_jaxpr/qgrd,kgd->qgrk/dot_general | solution.py:56
  246.2 5.3 %fusion.116 = f32[512,2]{0,1:T(2,128)S(1)} fusion(f32[512,2,4096]{2,0,1:T(8,128)S(1)} %get-tuple-element.478, f32[512,2]{0,1:T(2,128)S(1)} %get-tuple-element.480, pred[512,4096]{1,0:T(8,128)(4,1)S(1)} %fusion.113), kind=kLoop, calls=%fused_computation.41.clone.1 | loop fusion | flops 20970496 | bytes 18882560 | tf_op jit(solution)/shard_map/while/body/eval_jaxpr/reduce_sum | solution.py:64
  251.5 6.0 %fusion.118 = f32[1,512,1,2,128]{4,1,3,2,0:T(8,128)S(1)} fusion(f32[512,2,4096]{2,0,1:T(8,128)S(1)} %get-tuple-element.478, f32[512,2]{0,1:T(2,128)S(1)} %get-tuple-element.480, pred[512,4096]{1,0:T(8,128)(4,1)S(1)} %fusion.113, bf16[4096,1,128]{2,0,1:T(8,128)(2,1)S(1)} %copy-done.3, f32[2,512,1,2,128]{4,1,3,2,0:T(8,128)S(1)} %copy-done.6, ...), kind=kOutput, calls=%fused_computation.50.clone.1 | convolution fusion | flops 1094975488 | bytes 20979716 | tf_op jit(solution)/shard_map/while/body/eval_jaxpr/qgrk,kgd->qgrd/dot_general | solution.py:65
  257.6 1.2 copy_dynamic-update-slice_fusion.2
  258.8 0.2 copy.39
  259.0 1.2 div.34
  260.2 6.8 %convolution_convert_fusion = bf16[1024,4096]{1,0:T(8,128)(2,1)} fusion(bf16[256,4096]{1,0:T(8,128)(2,1)S(1)} %copy-done, f32[128,8,2,128]{3,2,1,0:T(2,128)S(1)} %bitcast.248, f32[128,8,2,128]{3,2,1,0:T(2,128)} %bitcast.249), kind=kOutput, calls=%fused_computation.74 | convolution fusion | flops 2152202240 | bytes 12582912 | tf_op jit(solution)/shard_map/dot_general | solution.py:214
  267.1 99.8 %reduce-scatter.2.cloned.1.call-done = bf16[64,4096]{1,0:T(8,128)(2,1)} async-done(((bf16[1024,4096]{1,0:T(8,128)(2,1)}), bf16[64,4096]{1,0:T(8,128)(2,1)}) %reduce-scatter.2.cloned.1.call-update) | async-done | bytes 524304 | tf_op jit(solution)/shard_map/reduce_scatter | solution.py:213
  (68 shorter events, 0.7 us)
Async XLA Ops:
  6.5 253.7 %copy-start = (bf16[256,4096]{1,0:T(8,128)(2,1)S(1)}, bf16[256,4096]{1,0:T(8,128)(2,1)}, u32[]{:S(2)}) copy-start(bf16[256,4096]{1,0:T(8,128)(2,1)} %param.16) | copy-start | bytes 6291460
  6.5 108.4 %all-gather.4.cloned.1.call-start = ((), (), s32[]{:S(2)}) async-start(), calls=%async_computation.1 | async-start | bytes 8912896 | tf_op jit(solution)/shard_map/all_gather | solution.py:118
  10.0 162.1 %all-gather.6.cloned.1.call-start = ((), (), s32[]{:S(2)}) async-start(), calls=%async_computation.2 | async-start | bytes 1114112 | tf_op jit(solution)/shard_map/all_gather | solution.py:183
  11.0 4.9 %collective-permute-start.3 = (bf16[256,2,64]{2,0,1:T(8,128)(2,1)S(1)}, bf16[256,2,64]{2,0,1:T(8,128)(2,1)S(1)}, u32[]{:S(2)}, u32[]{:S(2)}) collective-permute-start(bf16[256,2,64]{2,0,1:T(8,128)(2,1)S(1)} %bitcast.251), channel_id=1, source_target_pairs={{0,1},{1,0},{2,3},{3,2},{4,5},{5,4},{6,7},{7,6},{8,9},{9,8},{10,11... | collective-permute-start | bytes 196616 | tf_op jit(solution)/shard_map/ppermute | solution.py:18
  16.8 200.9 %all-gather.8.cloned.1.call-start = ((), (), s32[]{:S(2)}) async-start(), calls=%async_computation.3 | async-start | bytes 1114112 | tf_op jit(solution)/shard_map/all_gather | solution.py:184
  18.9 348.0 %reduce-scatter.2.cloned.1.call-start = ((), (), s32[]{:S(2)}) async-start(), calls=%async_computation.4 | async-start | bytes 8912896 | tf_op jit(solution)/shard_map/reduce_scatter | solution.py:213
  115.0 6.8 %copy-start.1 = (bf16[1024,4096]{1,0:T(8,128)(2,1)S(1)}, bf16[1024,4096]{1,0:T(8,128)(2,1)}, u32[]{:S(2)}) copy-start(bf16[1024,4096]{1,0:T(8,128)(2,1)} %all-gather.4.cloned.1.call-done) | copy-start | bytes 25165828
  115.0 6.8 %copy-start.2 = (bf16[4096,256]{1,0:T(8,128)(2,1)S(1)}, bf16[4096,256]{1,0:T(8,128)(2,1)}, u32[]{:S(2)}) copy-start(bf16[4096,256]{1,0:T(8,128)(2,1)} %param.14) | copy-start | bytes 6291460
  121.6 7.3 %collective-permute-start = (bf16[1024,2,64]{0,2,1:T(8,128)(2,1)S(1)}, bf16[1024,2,64]{0,2,1:T(8,128)(2,1)S(1)}, u32[]{:S(2)}, u32[]{:S(2)}) collective-permute-start(bf16[1024,2,64]{0,2,1:T(8,128)(2,1)S(1)} %bitcast.253), channel_id=1, source_target_pairs={{0,1},{1,0},{2,3},{3,2},{4,5},{5,4},{6,7},{7,6},{8,9},{9,8},{10,11... | collective-permute-start | bytes 786440 | tf_op jit(solution)/shard_map/ppermute | solution.py:18
  131.0 12.3 %collective-permute-start.1 = (bf16[1024,1,128]{0,2,1:T(8,128)(2,1)}, bf16[1024,1,128]{0,2,1:T(8,128)(2,1)}, u32[]{:S(2)}, u32[]{:S(2)}) collective-permute-start(bf16[1024,1,128]{0,2,1:T(8,128)(2,1)} %pad_maximum_fusion.2), channel_id=1, source_target_pairs={{0,16},{16,32},{32,48},{48,64},{64,80},{80,96},{96,112},{112,128},... | collective-permute-start | bytes 786440 | tf_op jit(solution)/shard_map/ppermute | solution.py:24
  138.4 6.9 %collective-permute-start.2 = (bf16[1024,1,128]{0,2,1:T(8,128)(2,1)S(1)}, bf16[1024,1,128]{0,2,1:T(8,128)(2,1)}, u32[]{:S(2)}, u32[]{:S(2)}) collective-permute-start(bf16[1024,1,128]{0,2,1:T(8,128)(2,1)S(1)} %get-tuple-element.302), channel_id=1, source_target_pairs={{0,16},{16,32},{32,48},{48,64},{64,80},{80,96},{96,112},{112,128},... | collective-permute-start | bytes 786440 | tf_op jit(solution)/shard_map/ppermute | solution.py:24
  148.8 6.2 %copy-start.4 = (f32[2,512,1,2,128]{4,1,3,2,0:T(8,128)S(1)}, f32[2,512,1,2,128]{4,1,3,2,0:T(8,128)}, u32[]{:S(2)}) copy-start(f32[2,512,1,2,128]{4,1,3,2,0:T(8,128)} %get-tuple-element.499) | copy-start | bytes 3145732 | tf_op jit(solution)/shard_map/while
  158.4 1.0 copy-start.5
  161.6 6.2 %copy-start.4 = (f32[2,512,1,2,128]{4,1,3,2,0:T(8,128)S(1)}, f32[2,512,1,2,128]{4,1,3,2,0:T(8,128)}, u32[]{:S(2)}) copy-start(f32[2,512,1,2,128]{4,1,3,2,0:T(8,128)} %get-tuple-element.499) | copy-start | bytes 3145732 | tf_op jit(solution)/shard_map/while
  171.1 1.0 copy-start.5
  225.7 5.3 %copy-start.3 = (bf16[4096,1,128]{2,0,1:T(8,128)(2,1)S(1)}, bf16[4096,1,128]{2,0,1:T(8,128)(2,1)}, u32[]{:S(2)}) copy-start(bf16[4096,1,128]{2,0,1:T(8,128)(2,1)} %get-tuple-element.557) | copy-start | bytes 3145732 | tf_op jit(solution)/shard_map/while
  225.7 5.3 %copy-start.6 = (f32[2,512,1,2,128]{4,1,3,2,0:T(8,128)S(1)}, f32[2,512,1,2,128]{4,1,3,2,0:T(8,128)}, u32[]{:S(2)}) copy-start(f32[2,512,1,2,128]{4,1,3,2,0:T(8,128)} %get-tuple-element.556) | copy-start | bytes 3145732 | tf_op jit(solution)/shard_map/while
  246.2 5.3 %copy-start.3 = (bf16[4096,1,128]{2,0,1:T(8,128)(2,1)S(1)}, bf16[4096,1,128]{2,0,1:T(8,128)(2,1)}, u32[]{:S(2)}) copy-start(bf16[4096,1,128]{2,0,1:T(8,128)(2,1)} %get-tuple-element.557) | copy-start | bytes 3145732 | tf_op jit(solution)/shard_map/while
  246.2 5.3 %copy-start.6 = (f32[2,512,1,2,128]{4,1,3,2,0:T(8,128)S(1)}, f32[2,512,1,2,128]{4,1,3,2,0:T(8,128)}, u32[]{:S(2)}) copy-start(f32[2,512,1,2,128]{4,1,3,2,0:T(8,128)} %get-tuple-element.556) | copy-start | bytes 3145732 | tf_op jit(solution)/shard_map/while
Sparse Core Ops, SparseCore 0:
  10.1 104.8 all-gather.3
  117.7 48.2 all-gather.5
  168.7 48.9 all-gather.7
  267.2 99.6 reduce-scatter.1
where the time goes:
time: 374 us; the launch traced here: 373 us
  waiting for transfers between devices  246 us (66%)
  matrix products  51.4 us (14%)
  other arithmetic  40.5 us (11%)
  between operations  13.4 us (4%)
  local copies, waits for them, and re-layouts  12.1 us (3%)
  starting transfers between devices  9.4 us (3%)
    reduce_scatter x1, waiting for transfers between devices, local(): lax.psum_scatter(jnp.dot(rows, w_out, preferred_element_type=jnp.float32)...  99.8 us
    all_gather x1, waiting for transfers between devices, local(): piece = lax.all_gather(normed, 'tp', axis=0, tiled=True)  96 us
    all_gather x1, waiting for transfers between devices, local(): piece_values = lax.all_gather(cache_values, 'grp', axis=0, tiled=True)  45.6 us
    dot_general x4, matrix products, fold_block(): jnp.einsum('qgrk,kgd->qgrd', weights.astype(jnp.bfloat16), values, prefer...  18.8 us
    dot_general x4, matrix products, fold_block(): jnp.einsum('qgrd,kgd->qgrk', queries, keys, preferred_element_type=jnp.fl...  16.7 us
    reduce_sum x4, other arithmetic, fold_block(): new_sum = run_sum * factor + jnp.sum(weights, axis=-1)  16.3 us
  transfers between devices with their start and end apart: 8, of which 5 were waited for; matrix products, arithmetic and copies ran while one was open for 13% of the time, Pallas kernels for 0%

commit v1 on v0

--- a/solution.py
+++ b/solution.py
@@ -2,6 +2,7 @@
 import jax.numpy as jnp
 from jax import lax
 from jax.sharding import PartitionSpec as P
+from jax.lax import all_to_all, axis_size
 
 KVH = 8
 HD = 128
@@ -115,7 +116,16 @@
     inverse = lax.rsqrt(variance)
     normed = (wide * inverse * norm_gain).astype(jnp.bfloat16)
     kv_weight = w_keyval.reshape(w_keyval.shape[0], 2 * kv_cols)
-    piece = lax.all_gather(normed, "tp", axis=0, tiled=True)
+
+    def search_the_sector(piece_in, across):
+        return jnp.concatenate(
+            all_to_all(
+                jnp.stack([piece_in for _ in range(axis_size(across))], axis=0), across, 0, 0
+            ),
+            axis=0,
+        )
+
+    piece = search_the_sector(normed, "tp")
     query_part = jnp.dot(piece, w_query, preferred_element_type=jnp.float32)
     kv_part = jnp.dot(piece, kv_weight, preferred_element_type=jnp.float32)
     projected = jnp.concatenate([query_part, kv_part], axis=1)

time: 374 us -> 477 us (1.28)
  waiting for transfers between devices: 246 us -> 329 us
  starting transfers between devices: 9.4 us -> 21 us
  local copies, waits for them, and re-layouts: 12.1 us -> 20.2 us
    ppermute x2, waiting for transfers between devices: 4.8 us -> 186 us  [swapped(): return lax.ppermute(block, axis, route)]
    all_gather x1 -> x0, waiting for transfers between devices: 96 us -> none  [local(): piece = lax.all_gather(normed, 'tp', axis=0, tiled=True)]
    all_to_all x0 -> x1, starting transfers between devices: none -> 10.3 us  [search_the_sector(): all_to_all(jnp.stack([piece_in for _ in range(axis_size(across))], axis=0...]
  transfers between devices with their start and end apart: 8 -> 8, of which waited for: 5 -> 4; matrix products, arithmetic and copies ran while one was open for 13% -> 11% of each run, Pallas kernels for 0% -> 0%
where the time goes in v1:
time: 477 us
  waiting for transfers between devices  329 us (69%)
  matrix products  54.7 us (11%)
  other arithmetic  37.7 us (8%)
  starting transfers between devices  21 us (4%)
  local copies, waits for them, and re-layouts  20.2 us (4%)
  between operations  13.4 us (3%)
    ppermute x2, waiting for transfers between devices, swapped(): return lax.ppermute(block, axis, route)  186 us
    reduce_scatter x1, waiting for transfers between devices, local(): lax.psum_scatter(jnp.dot(rows, w_out, preferred_element_type=jnp.float32)...  99.8 us
    all_gather x1, waiting for transfers between devices, local(): piece_values = lax.all_gather(cache_values, 'grp', axis=0, tiled=True)  42.6 us
    dot_general x4, matrix products, fold_block(): jnp.einsum('qgrk,kgd->qgrd', weights.astype(jnp.bfloat16), values, prefer...  18.7 us
    dot_general x4, matrix products, fold_block(): jnp.einsum('qgrd,kgd->qgrk', queries, keys, preferred_element_type=jnp.fl...  16.5 us
    reduce_sum x4, other arithmetic, fold_block(): new_sum = run_sum * factor + jnp.sum(weights, axis=-1)  16.3 us
    all_to_all x1, starting transfers between devices, search_the_sector(): all_to_all(jnp.stack([piece_in for _ in range(axis_size(across))], axis=0...  10.3 us
  transfers between devices with their start and end apart: 8, of which 4 were waited for; matrix products, arithmetic and copies ran while one was open for 11% of the time, Pallas kernels for 0%

profile of v1, /device:TPU:1, one launch (start us, length us, event | category | flops | bytes accessed | tf_op | source)
XLA Modules:
  0.0 476.7 jit_solution(3717066883120584008)
XLA Ops:
  6.5 1.4 fusion.67
  7.9 1.2 fusion.69
  9.2 4.3 stack.2
  13.5 10.3 %all-to-all-start = ((bf16[16,64,4096]{2,1,0:T(8,128)(2,1)}), bf16[16,64,4096]{2,1,0:T(8,128)(2,1)}, u32[]{:S(2)}, u32[]{:S(2)}) async-start(bf16[16,64,4096]{2,1,0:T(8,128)(2,1)} %stack.2), calls=%async_computation | async-start | bytes 16777216 | tf_op jit(solution)/shard_map/all_to_all | solution.py:122
  23.9 0.1 copy.43
  24.0 1.4 collective-permute-start.3
  25.4 0.3 convert_reduce_fusion
  25.7 0.1 copy.37
  25.8 0.1 reduce.4
  26.0 0.1 dynamic-slice_select_fusion
  26.1 185.8 %collective-permute-done.3 = bf16[256,2,64]{2,0,1:T(8,128)(2,1)S(1)} collective-permute-done((bf16[256,2,64]{2,0,1:T(8,128)(2,1)S(1)}, bf16[256,2,64]{2,0,1:T(8,128)(2,1)S(1)}, u32[]{:S(2)}, u32[]{:S(2)}) %collective-permute-start.3) | collective-permute-done | bytes 65568 | tf_op jit(solution)/shard_map/ppermute | solution.py:19
  211.9 0.1 maximum_select_fusion.1
  212.0 0.7 fusion.82
  212.8 0.1 select_reduce_fusion
  213.0 4.2 copy.46
  217.2 0.1 select_reduce_fusion.2
  217.4 1.0 multiply_cosine_fusion.1
  218.4 6.7 %convolution_convert_fusion.1 = bf16[1024,128]{0,1:T(8,128)(2,1)S(1)} fusion(bf16[1024,4096]{1,0:T(8,128)(2,1)} %bitcast.19, bf16[4096,128]{0,1:T(8,128)(2,1)} %bitcast.266), kind=kOutput, calls=%fused_computation.79 | convolution fusion | flops 1073872896 | bytes 9699328 | tf_op jit(solution)/shard_map/dot_general | solution.py:130
  225.1 2.3 collective-permute-start
  227.4 6.1 %fusion.83 = f32[1024,2,128]{0,2,1:T(8,128)S(1)} fusion(bf16[1024,4096,1]{1,0,2:T(8,128)(2,1)} %bitcast.20, bf16[2,128,4096]{2,1,0:T(8,128)(2,1)S(1)} %bitcast.254), kind=kOutput, calls=%fused_computation.128 | convolution fusion | flops 2147483648 | bytes 11534336 | tf_op jit(solution)/shard_map/dot_general | solution.py:129
  233.5 0.1 maximum_select_fusion
  233.6 0.8 fusion.81
  234.4 1.1 fusion.77
  235.5 0.7 pad_maximum_fusion.2
  236.3 4.8 %collective-permute-start.1 = (bf16[1024,1,128]{0,2,1:T(8,128)(2,1)}, bf16[1024,1,128]{0,2,1:T(8,128)(2,1)}, u32[]{:S(2)}, u32[]{:S(2)}) collective-permute-start(bf16[1024,1,128]{0,2,1:T(8,128)(2,1)} %pad_maximum_fusion.2), channel_id=1, source_target_pairs={{0,16},{16,32},{32,48},{48,64},{64,80},{80,96},{96,112},{112,128},... | collective-permute-start | bytes 786440 | tf_op jit(solution)/shard_map/ppermute | solution.py:25
  241.1 0.9 subtract_convert_fusion
  242.0 1.1 concatenate.58
  243.1 0.3 copy.40
  243.4 0.9 concatenate.57
  244.3 1.2 copy.39
  245.6 2.1 collective-permute-start.2
  247.7 1.1 pad_maximum_fusion
  248.8 1.0 maximum_maximum_fusion
  249.8 0.3 copy.41
  250.0 1.1 collective-permute-done.2
  251.1 1.1 pad_maximum_fusion.1
  252.2 1.0 copy.42
  253.2 25.2 %while.27 = (s32[]{:T(128)}, f32[2,512,1,2]{1,3,2,0:T(2,128)S(1)}, f32[2,512,1,2]{1,3,2,0:T(2,128)S(1)}, f32[2,512,1,2,128]{4,1,3,2,0:T(8,128)}, s32[2048]{0:T(1...) while((s32[]{:T(128)}, f32[2,512,1,2]{1,3,2,0:T(2,128)S(1)}, ...), condition=%wide.region_8.9_spmd, body=%wide.region_5.8_spmd.sunk | while | flops 1108483072 | bytes 41785588 | solution.py:93
  253.2 2.1 fusion.106
  255.4 3.1 fusion.107
  258.5 2.9 fusion.108
  261.4 3.4 fusion.110
  264.8 1.0 copy-done.8
  265.9 2.1 fusion.106
  268.0 3.1 fusion.107
  271.1 2.9 fusion.108
  274.1 3.4 fusion.110
  277.4 1.0 copy-done.8
  278.4 42.6 %all-gather.5.cloned.1.call-done = bf16[4096,1,128]{2,0,1:T(8,128)(2,1)} async-done(((bf16[256,1,128]{2,0,1:T(8,128)(2,1)}), bf16[4096,1,128]{2,0,1:T(8,128)(2,1)}) %all-gather.5.cloned.1.call-update) | async-done | bytes 1048592 | tf_op jit(solution)/shard_map/all_gather | solution.py:194
  321.0 41.1 %while.28 = (s32[]{:T(128)}, f32[2,512,1,2]{1,3,2,0:T(2,128)S(1)}, f32[2,512,1,2,128]{4,3,1,0,2:T(2,128)}, f32[2,512,1,2]{1,3,2,0:T(2,128)S(1)}, f32[2,512,1,2]{...) while((s32[]{:T(128)}, f32[2,512,1,2]{1,3,2,0:T(2,128)S(1)}, ...), condition=%wide.region_13.14_spmd.clone, body=%wide.region_10.13_spmd.clone.sunk | while | flops 2212773888 | bytes 71670216 | solution.py:93
  321.2 2.6 fusion.113
  323.8 5.1 %fusion.114 = (f32[512,2]{0,1:T(2,128)S(1)}, f32[512,2,4096]{2,0,1:T(8,128)S(1)}) fusion(pred[512,4096]{1,0:T(8,128)(4,1)S(1)} %fusion.113, bf16[4096,1,128]{2,0,1:T(8,128)(2,1)} %get-tuple-element.496, bf16[2,512,1,2,128]{4,1,3,2,0:T(8,128)(2,1)} %get-tuple-element.495, s32[]{:T(128)S(6)} %copy.79), kind=kOutput, calls=%fused_computation.39.clone.1 | convolution fusion | flops 1086323712 | bytes 20189188 | tf_op jit(solution)/shard_map/while/body/eval_jaxpr/qgrd,kgd->qgrk/dot_general | solution.py:57
  329.0 5.3 %fusion.116 = f32[512,2]{0,1:T(2,128)S(1)} fusion(f32[512,2,4096]{2,0,1:T(8,128)S(1)} %get-tuple-element.419, f32[512,2]{0,1:T(2,128)S(1)} %get-tuple-element.421, pred[512,4096]{1,0:T(8,128)(4,1)S(1)} %fusion.113), kind=kLoop, calls=%fused_computation.41.clone.1 | loop fusion | flops 20970496 | bytes 18882560 | tf_op jit(solution)/shard_map/while/body/eval_jaxpr/reduce_sum | solution.py:65
  334.3 6.0 %fusion.118 = f32[1,512,1,2,128]{4,1,3,2,0:T(8,128)S(1)} fusion(f32[512,2,4096]{2,0,1:T(8,128)S(1)} %get-tuple-element.419, f32[512,2]{0,1:T(2,128)S(1)} %get-tuple-element.421, pred[512,4096]{1,0:T(8,128)(4,1)S(1)} %fusion.113, bf16[4096,1,128]{2,0,1:T(8,128)(2,1)S(1)} %copy-done.5, f32[2,512,1,2,128]{4,1,3,2,0:T(8,128)S(1)} %copy-done.9, ...), kind=kOutput, calls=%fused_computation.50.clone.1 | convolution fusion | flops 1094975488 | bytes 20979716 | tf_op jit(solution)/shard_map/while/body/eval_jaxpr/qgrk,kgd->qgrd/dot_general | solution.py:66
  340.3 1.2 copy_dynamic-update-slice_fusion.2
  341.7 2.6 fusion.113
  344.3 5.1 %fusion.114 = (f32[512,2]{0,1:T(2,128)S(1)}, f32[512,2,4096]{2,0,1:T(8,128)S(1)}) fusion(pred[512,4096]{1,0:T(8,128)(4,1)S(1)} %fusion.113, bf16[4096,1,128]{2,0,1:T(8,128)(2,1)} %get-tuple-element.496, bf16[2,512,1,2,128]{4,1,3,2,0:T(8,128)(2,1)} %get-tuple-element.495, s32[]{:T(128)S(6)} %copy.79), kind=kOutput, calls=%fused_computation.39.clone.1 | convolution fusion | flops 1086323712 | bytes 20189188 | tf_op jit(solution)/shard_map/while/body/eval_jaxpr/qgrd,kgd->qgrk/dot_general | solution.py:57
  349.5 5.3 %fusion.116 = f32[512,2]{0,1:T(2,128)S(1)} fusion(f32[512,2,4096]{2,0,1:T(8,128)S(1)} %get-tuple-element.419, f32[512,2]{0,1:T(2,128)S(1)} %get-tuple-element.421, pred[512,4096]{1,0:T(8,128)(4,1)S(1)} %fusion.113), kind=kLoop, calls=%fused_computation.41.clone.1 | loop fusion | flops 20970496 | bytes 18882560 | tf_op jit(solution)/shard_map/while/body/eval_jaxpr/reduce_sum | solution.py:65
  354.8 6.0 %fusion.118 = f32[1,512,1,2,128]{4,1,3,2,0:T(8,128)S(1)} fusion(f32[512,2,4096]{2,0,1:T(8,128)S(1)} %get-tuple-element.419, f32[512,2]{0,1:T(2,128)S(1)} %get-tuple-element.421, pred[512,4096]{1,0:T(8,128)(4,1)S(1)} %fusion.113, bf16[4096,1,128]{2,0,1:T(8,128)(2,1)S(1)} %copy-done.5, f32[2,512,1,2,128]{4,1,3,2,0:T(8,128)S(1)} %copy-done.9, ...), kind=kOutput, calls=%fused_computation.50.clone.1 | convolution fusion | flops 1094975488 | bytes 20979716 | tf_op jit(solution)/shard_map/while/body/eval_jaxpr/qgrk,kgd->qgrd/dot_general | solution.py:66
  360.9 1.2 copy_dynamic-update-slice_fusion.2
  362.1 0.2 copy.45
  362.3 1.2 div.34
  363.5 6.8 %convolution_convert_fusion = bf16[1024,4096]{1,0:T(8,128)(2,1)} fusion(bf16[256,4096]{1,0:T(8,128)(2,1)S(1)} %copy-done, f32[128,8,2,128]{3,2,1,0:T(2,128)S(1)} %bitcast.252, f32[128,8,2,128]{3,2,1,0:T(2,128)} %bitcast.255), kind=kOutput, calls=%fused_computation.74 | convolution fusion | flops 2152202240 | bytes 12582912 | tf_op jit(solution)/shard_map/dot_general | solution.py:224
  370.4 99.8 %reduce-scatter.2.cloned.1.call-done = bf16[64,4096]{1,0:T(8,128)(2,1)} async-done(((bf16[1024,4096]{1,0:T(8,128)(2,1)}), bf16[64,4096]{1,0:T(8,128)(2,1)}) %reduce-scatter.2.cloned.1.call-update) | async-done | bytes 524304 | tf_op jit(solution)/shard_map/reduce_scatter | solution.py:223
  (78 shorter events, 0.9 us)
Async XLA Ops:
  6.5 357.0 %copy-start = (bf16[256,4096]{1,0:T(8,128)(2,1)S(1)}, bf16[256,4096]{1,0:T(8,128)(2,1)}, u32[]{:S(2)}) copy-start(bf16[256,4096]{1,0:T(8,128)(2,1)} %param.16) | copy-start | bytes 6291460
  13.5 10.4 %copy-start.4 = (bf16[2,128,2,64]{1,3,2,0:T(8,128)(2,1)S(1)}, bf16[2,128,2,64]{1,3,2,0:T(8,128)(2,1)}, u32[]{:S(2)}) copy-start(bf16[2,128,2,64]{1,3,2,0:T(8,128)(2,1)} %param.17) | copy-start | bytes 196612
  13.5 11.9 %copy-start.3 = (s32[16384]{0:T(1024)S(1)}, s32[16384]{0:T(1024)}, u32[]{:S(2)}) copy-start(s32[16384]{0:T(1024)} %param.19) | copy-start | bytes 196612
  13.5 203.8 %copy-start.6 = (s32[32]{0:T(128)S(1)}, s32[32]{0:T(128)}, u32[]{:S(2)}) copy-start(s32[32]{0:T(128)} %param.18) | copy-start | bytes 388
  13.5 205.0 %all-to-all-start = ((bf16[16,64,4096]{2,1,0:T(8,128)(2,1)}), bf16[16,64,4096]{2,1,0:T(8,128)(2,1)}, u32[]{:S(2)}, u32[]{:S(2)}) async-start(bf16[16,64,4096]{2,1,0:T(8,128)(2,1)} %stack.2), calls=%async_computation | async-start | bytes 16777216 | tf_op jit(solution)/shard_map/all_to_all | solution.py:122
  23.8 254.6 %all-gather.3.cloned.1.call-start = ((), (), s32[]{:S(2)}) async-start(), calls=%async_computation.2 | async-start | bytes 1114112 | tf_op jit(solution)/shard_map/all_gather | solution.py:193
  24.0 187.9 %collective-permute-start.3 = (bf16[256,2,64]{2,0,1:T(8,128)(2,1)S(1)}, bf16[256,2,64]{2,0,1:T(8,128)(2,1)S(1)}, u32[]{:S(2)}, u32[]{:S(2)}) collective-permute-start(bf16[256,2,64]{2,0,1:T(8,128)(2,1)S(1)} %bitcast.256), channel_id=1, source_target_pairs={{0,1},{1,0},{2,3},{3,2},{4,5},{5,4},{6,7},{7,6},{8,9},{9,8},{10,11... | collective-permute-start | bytes 196616 | tf_op jit(solution)/shard_map/ppermute | solution.py:19
  212.7 108.3 %all-gather.5.cloned.1.call-start = ((), (), s32[]{:S(2)}) async-start(), calls=%async_computation.3 | async-start | bytes 1114112 | tf_op jit(solution)/shard_map/all_gather | solution.py:194
  218.4 251.8 %reduce-scatter.2.cloned.1.call-start = ((), (), s32[]{:S(2)}) async-start(), calls=%async_computation.4 | async-start | bytes 8912896 | tf_op jit(solution)/shard_map/reduce_scatter | solution.py:223
  218.4 9.0 %copy-start.1 = (bf16[256,4096]{1,0:T(8,128)(2,1)S(1)}, bf16[256,4096]{1,0:T(8,128)(2,1)}, u32[]{:S(2)}) copy-start(bf16[256,4096]{1,0:T(8,128)(2,1)} %copy.46) | copy-start | bytes 6291460
  225.1 8.4 %collective-permute-start = (bf16[1024,2,64]{0,2,1:T(8,128)(2,1)S(1)}, bf16[1024,2,64]{0,2,1:T(8,128)(2,1)S(1)}, u32[]{:S(2)}, u32[]{:S(2)}) collective-permute-start(bf16[1024,2,64]{0,2,1:T(8,128)(2,1)S(1)} %bitcast.258), channel_id=1, source_target_pairs={{0,1},{1,0},{2,3},{3,2},{4,5},{5,4},{6,7},{7,6},{8,9},{9,8},{10,11... | collective-permute-start | bytes 786440 | tf_op jit(solution)/shard_map/ppermute | solution.py:19
  236.3 12.5 %collective-permute-start.1 = (bf16[1024,1,128]{0,2,1:T(8,128)(2,1)}, bf16[1024,1,128]{0,2,1:T(8,128)(2,1)}, u32[]{:S(2)}, u32[]{:S(2)}) collective-permute-start(bf16[1024,1,128]{0,2,1:T(8,128)(2,1)} %pad_maximum_fusion.2), channel_id=1, source_target_pairs={{0,16},{16,32},{32,48},{48,64},{64,80},{80,96},{96,112},{112,128},... | collective-permute-start | bytes 786440 | tf_op jit(solution)/shard_map/ppermute | solution.py:25
  245.6 5.5 %collective-permute-start.2 = (bf16[1024,1,128]{0,2,1:T(8,128)(2,1)}, bf16[1024,1,128]{0,2,1:T(8,128)(2,1)}, u32[]{:S(2)}, u32[]{:S(2)}) collective-permute-start(bf16[1024,1,128]{0,2,1:T(8,128)(2,1)} %get-tuple-element.243), channel_id=1, source_target_pairs={{0,16},{16,32},{32,48},{48,64},{64,80},{80,96},{96,112},{112,128},... | collective-permute-start | bytes 786440 | tf_op jit(solution)/shard_map/ppermute | solution.py:25
  255.4 6.0 %copy-start.2 = (bf16[2048,1,128]{2,0,1:T(8,128)(2,1)S(1)}, bf16[2048,1,128]{2,0,1:T(8,128)(2,1)}, u32[]{:S(2)}) copy-start(bf16[2048,1,128]{2,0,1:T(8,128)(2,1)} %get-tuple-element.463) | copy-start | bytes 1572868 | tf_op jit(solution)/shard_map/while
  255.4 6.0 %copy-start.7 = (f32[2,512,1,2,128]{4,1,3,2,0:T(8,128)S(1)}, f32[2,512,1,2,128]{4,1,3,2,0:T(8,128)}, u32[]{:S(2)}) copy-start(f32[2,512,1,2,128]{4,1,3,2,0:T(8,128)} %get-tuple-element.440) | copy-start | bytes 3145732 | tf_op jit(solution)/shard_map/while
  264.8 1.0 copy-start.8
  268.0 6.0 %copy-start.2 = (bf16[2048,1,128]{2,0,1:T(8,128)(2,1)S(1)}, bf16[2048,1,128]{2,0,1:T(8,128)(2,1)}, u32[]{:S(2)}) copy-start(bf16[2048,1,128]{2,0,1:T(8,128)(2,1)} %get-tuple-element.463) | copy-start | bytes 1572868 | tf_op jit(solution)/shard_map/while
  268.0 6.0 %copy-start.7 = (f32[2,512,1,2,128]{4,1,3,2,0:T(8,128)S(1)}, f32[2,512,1,2,128]{4,1,3,2,0:T(8,128)}, u32[]{:S(2)}) copy-start(f32[2,512,1,2,128]{4,1,3,2,0:T(8,128)} %get-tuple-element.440) | copy-start | bytes 3145732 | tf_op jit(solution)/shard_map/while
  277.4 1.0 copy-start.8
  329.0 5.3 %copy-start.5 = (bf16[4096,1,128]{2,0,1:T(8,128)(2,1)S(1)}, bf16[4096,1,128]{2,0,1:T(8,128)(2,1)}, u32[]{:S(2)}) copy-start(bf16[4096,1,128]{2,0,1:T(8,128)(2,1)} %get-tuple-element.498) | copy-start | bytes 3145732 | tf_op jit(solution)/shard_map/while
  329.0 5.3 %copy-start.9 = (f32[2,512,1,2,128]{4,1,3,2,0:T(8,128)S(1)}, f32[2,512,1,2,128]{4,1,3,2,0:T(8,128)}, u32[]{:S(2)}) copy-start(f32[2,512,1,2,128]{4,1,3,2,0:T(8,128)} %get-tuple-element.497) | copy-start | bytes 3145732 | tf_op jit(solution)/shard_map/while
  349.5 5.3 %copy-start.5 = (bf16[4096,1,128]{2,0,1:T(8,128)(2,1)S(1)}, bf16[4096,1,128]{2,0,1:T(8,128)(2,1)}, u32[]{:S(2)}) copy-start(bf16[4096,1,128]{2,0,1:T(8,128)(2,1)} %get-tuple-element.498) | copy-start | bytes 3145732 | tf_op jit(solution)/shard_map/while
  349.5 5.3 %copy-start.9 = (f32[2,512,1,2,128]{4,1,3,2,0:T(8,128)S(1)}, f32[2,512,1,2,128]{4,1,3,2,0:T(8,128)}, u32[]{:S(2)}) copy-start(f32[2,512,1,2,128]{4,1,3,2,0:T(8,128)} %get-tuple-element.497) | copy-start | bytes 3145732 | tf_op jit(solution)/shard_map/while
Sparse Core Ops, SparseCore 0:
  212.9 54.7 all-gather.2
  270.4 50.5 all-gather.4
  370.5 99.6 reduce-scatter.1
